TPU v7x, 32 devices: a whole 2x2x4 slice. The times are simulated.
32 devices in a mesh: grp: 16 (over z, x, core), gy: 2 (over y).
Axes of the slice: x: 2, y: 2, z: 4, core: 2. Of those that a mesh axis runs over, the one named last changes fastest.
Arguments:
- potential_warmth: float32 [24, 256, 1024], P(None, 'grp', 'gy'), may hold values from -2 to 4
- saltiness_anomaly: float32 [24, 256, 1024], P(None, 'grp', 'gy'), may hold values from -6 to 6
- seawater_velocity: float32 [2, 256, 1024], P(None, 'grp', 'gy'), may hold values from -2 to 2
- airflow_surface_forcing: float32 [2, 256, 1024], P(None, 'grp', 'gy'), may hold values from -3 to 3
- glacial_velocity_sigma: float32 [5, 256, 1024], P(None, 'grp', 'gy'), may hold values from -3 to 3
- category_coverage: float32 [5, 256, 1024], P(None, 'grp', 'gy'), may hold values from 0.17 to 0.2
- category_thickness: float32 [5, 256, 1024], P(None, 'grp', 'gy'), may hold values from 0.2 to 1
- seawater_indicator: int32 [256, 1024], P('grp', 'gy'), may hold values from 0 to 1
- dynamics_indicator: int32 [256, 1024], P('grp', 'gy'), may hold values from 0 to 1, as said below
- patch_home_position: int32 [16, 8], P('grp', 'gy'), may hold values from -1 to 3, as said below
Outputs:
- potential_warmth_updated: float32 [24, 256, 1024], P(None, 'grp', 'gy')
- saltiness_updated: float32 [24, 256, 1024], P(None, 'grp', 'gy')
- coupled_surface_velocity: float32 [2, 256, 1024], P(None, 'grp', 'gy')
- glacial_patch_update: float32 [5, 256, 1024], P(None, 'grp', 'gy')
Inputs may be any that keep to these rules, and one draw needn't show every extreme that they name: For a block with ice, patch_home_position = d * 2 + p: it goes to slot p from its tile of the device with the same grp index and gy index d; no two blocks of one tile share a value; the first tile row holds 4 blocks with ice in every draw. `dynamics_indicator`: 1 only at cells with seawater_indicator 1 inside blocks whose patch_home_position is not negative.
All inputs are finite; a program needn't handle non-finite values.
Results may differ from a plain program's by a relative error of at most 0.0003.
Values sent between devices are 32-bit elements; how exact they have to be, the bound alone decides.
A program may use at most 64 MiB of HBM per device.

v0:
```python
import jax
import jax.numpy as jnp
from jax import lax
from jax.sharding import PartitionSpec as P

NSUB = 4


DIFFUSIVITY = 0.2
STRENGTH_COEF = 20.0
MIN_MASS = 0.5
RELAX_RATE = 0.5
ECCENTRIC = 4.0
DELTA_FLOOR = 0.0025
SPEED_FLOOR = 0.01
CORIOLIS = 0.5
HEAT_COEF = 4.0
THIN_LIMIT = 0.1
FREEZING = -1.8
WARMTH_FACTOR = 0.05
STRESS_SCALE = 0.5


def extended(cells, sides, width):
    for axis, dim in sides:
        count = lax.axis_size(axis)
        head = lax.slice_in_dim(cells, 0, width, axis=dim)
        tail = lax.slice_in_dim(cells, cells.shape[dim] - width, cells.shape[dim], axis=dim)
        cells = jnp.concatenate(
            [
                lax.ppermute(tail, axis, [(i, (i + 1) % count) for i in range(count)]),
                cells,
                lax.ppermute(head, axis, [((i + 1) % count, i) for i in range(count)]),
            ],
            axis=dim,
        )
    return cells


def east_of(field, offset):
    return jnp.roll(field, -offset, axis=-2)


def north_of(field, offset):
    border = jnp.zeros_like(field[..., :1])
    if offset > 0:
        return jnp.concatenate([field[..., 1:], border], axis=-1)
    return jnp.concatenate([border, field[..., :-1]], axis=-1)


def evp_subcycles(
    vel_u,
    vel_v,
    sig_one,
    sig_two,
    sig_shear,
    cur_u,
    cur_v,
    concentration,
    thickness,
    wind_u,
    wind_v,
    glacial_indicator,
):
    strength = thickness * jnp.exp(-STRENGTH_COEF * (1.0 - concentration))
    ice_mass = thickness + MIN_MASS
    for subcycle in range(NSUB):
        u_east = east_of(vel_u, 1) - vel_u
        v_north = north_of(vel_v, 1) - vel_v
        u_north = north_of(vel_u, 1) - vel_u
        v_east = east_of(vel_v, 1) - vel_v
        divergence = u_east + v_north
        tension = u_east - v_north
        shear_rate = u_north + v_east
        deform_rate = jnp.sqrt(
            divergence * divergence
            + (tension * tension + shear_rate * shear_rate) / ECCENTRIC
            + DELTA_FLOOR
        )
        viscous = strength / deform_rate
        sig_one = (
            glacial_indicator
            * (sig_one + RELAX_RATE * (viscous * divergence - strength))
            / (1.0 + RELAX_RATE)
        )
        sig_two = (
            glacial_indicator
            * (sig_two + RELAX_RATE * viscous * tension / ECCENTRIC)
            / (1.0 + RELAX_RATE)
        )
        sig_shear = (
            glacial_indicator
            * (sig_shear + RELAX_RATE * viscous * shear_rate / ECCENTRIC)
            / (1.0 + RELAX_RATE)
        )
        back_one_x = sig_one - east_of(sig_one, -1)
        back_two_x = sig_two - east_of(sig_two, -1)
        back_one_y = sig_one - north_of(sig_one, -1)
        back_two_y = sig_two - north_of(sig_two, -1)
        force_u = 0.5 * (back_one_x + back_two_x) + (sig_shear - north_of(sig_shear, -1))
        force_v = 0.5 * (back_one_y - back_two_y) + (sig_shear - east_of(sig_shear, -1))
        rel_speed = jnp.sqrt((cur_u - vel_u) ** 2 + (cur_v - vel_v) ** 2 + SPEED_FLOOR)
        water_coef = concentration * rel_speed
        implicit = ice_mass + water_coef
        new_u = (
            glacial_indicator
            * (
                ice_mass * vel_u
                + force_u
                + wind_u
                + water_coef * cur_u
                + CORIOLIS * ice_mass * vel_v
            )
            / implicit
        )
        new_v = (
            glacial_indicator
            * (
                ice_mass * vel_v
                + force_v
                + wind_v
                + water_coef * cur_v
                - CORIOLIS * ice_mass * vel_u
            )
            / implicit
        )
        vel_u, vel_v = (new_u, new_v)
    rel_speed = jnp.sqrt((cur_u - vel_u) ** 2 + (cur_v - vel_v) ** 2 + SPEED_FLOOR)
    water_coef = concentration * rel_speed
    stress_u = glacial_indicator * water_coef * (vel_u - cur_u)
    stress_v = glacial_indicator * water_coef * (vel_v - cur_v)
    return ((vel_u, vel_v, sig_one, sig_two, sig_shear), (stress_u, stress_v))


def seabed_exchange(
    surface_temp, category_coverage, category_thickness, glacial_indicator, cat_axis
):
    denominator = category_thickness + THIN_LIMIT * category_coverage
    denominator = jnp.where(denominator > 0.0, denominator, 1.0)
    per_cat = HEAT_COEF * category_coverage * category_coverage / denominator
    return glacial_indicator * (surface_temp - FREEZING) * jnp.sum(per_cat, axis=cat_axis)


def close_rims(padded, width):
    lat_index = lax.axis_index("gy")
    groups = lax.axis_size("gy")
    columns = jnp.arange(padded.shape[-1])
    low_rim = (columns < width) & (lat_index == 0)
    high_rim = (columns >= padded.shape[-1] - width) & (lat_index == groups - 1)
    return jnp.where(low_rim | high_rim, 0.0, padded)


def diffuse_tile(wide):
    fields = wide[:-1]
    wet_wide = wide[-1]
    centre = fields[:, 1:-1, 1:-1]
    inflow = jnp.zeros_like(centre)
    for row_cut, col_cut in (
        (slice(2, None), slice(1, -1)),
        (slice(None, -2), slice(1, -1)),
        (slice(1, -1), slice(2, None)),
        (slice(1, -1), slice(None, -2)),
    ):
        inflow = inflow + wet_wide[row_cut, col_cut] * (fields[:, row_cut, col_cut] - centre)
    return centre + DIFFUSIVITY * wet_wide[1:-1, 1:-1] * inflow


def interior(field):
    return field[..., NSUB : field.shape[-2] - NSUB, NSUB : field.shape[-1] - NSUB]


def run_blocks(windows):
    state, stress = evp_subcycles(*[windows[:, :, plane_number] for plane_number in range(12)])
    owned_state = jnp.stack([interior(member) for member in state], axis=2)
    return (owned_state, [interior(member) for member in stress])


def per_device(
    potential_warmth,
    saltiness_anomaly,
    seawater_velocity,
    airflow_surface_forcing,
    glacial_velocity_sigma,
    category_coverage,
    category_thickness,
    seawater_indicator,
    dynamics_indicator,
    patch_home_position,
):
    vertical_count_value = potential_warmth.shape[0]
    patch_east_count = potential_warmth.shape[1]
    patch_north_count = potential_warmth.shape[2]
    nblock = patch_home_position.shape[1]
    block_len = patch_north_count // nblock
    groups = lax.axis_size("gy")
    pair_count = nblock // groups
    seawater_points = seawater_indicator.astype(jnp.float32)
    glacial_indicator = dynamics_indicator.astype(jnp.float32)
    concentration = jnp.sum(category_coverage, axis=0)
    thickness = jnp.sum(category_thickness, axis=0)
    quantity_stack = jnp.concatenate(
        [potential_warmth, saltiness_anomaly, seawater_points[None]], axis=0
    )
    ice_stack = jnp.concatenate(
        [
            glacial_velocity_sigma,
            seawater_velocity,
            concentration[None],
            thickness[None],
            airflow_surface_forcing,
            glacial_indicator[None],
        ],
        axis=0,
    )
    tracer_wide = close_rims(extended(quantity_stack, (("grp", 1), ("gy", 2)), 1), 1)
    ice_wide = close_rims(extended(ice_stack, (("grp", 1), ("gy", 2)), NSUB), NSUB)
    smoothed_field = diffuse_tile(tracer_wide)
    windows = jnp.stack(
        [
            ice_wide[
                :, :, block_number * block_len : block_number * block_len + block_len + 2 * NSUB
            ]
            for block_number in range(nblock)
        ],
        axis=0,
    )
    chooser = (
        patch_home_position[0][None, :] == jnp.arange(nblock, dtype=jnp.int32)[:, None]
    ).astype(jnp.float32)
    local_state, local_stress = run_blocks(windows[:, None])
    stress_fields = jnp.stack([local_stress[0][:, 0], local_stress[1][:, 0]], axis=1)
    stress_fields = stress_fields.transpose(1, 2, 0, 3).reshape(
        2, patch_east_count, patch_north_count
    )
    picked = jnp.einsum(
        "sb,bfxy->sfxy", chooser, local_state[:, 0], precision=lax.Precision.HIGHEST
    )
    owned_state = lax.all_to_all(
        picked.reshape((groups, pair_count) + picked.shape[1:]),
        "gy",
        split_axis=0,
        concat_axis=0,
        tiled=True,
    )
    heat_exchange = seabed_exchange(
        potential_warmth[0], category_coverage, category_thickness, glacial_indicator, 0
    )
    potential_warmth_updated = smoothed_field[:vertical_count_value]
    potential_warmth_updated = potential_warmth_updated.at[0].add(
        -WARMTH_FACTOR * seawater_points * heat_exchange
    )
    saltiness_updated = smoothed_field[vertical_count_value : 2 * vertical_count_value]
    coupled_surface_velocity = seawater_points * (seawater_velocity + STRESS_SCALE * stress_fields)
    glacial_patch_update = (
        owned_state.reshape(nblock, 5, patch_east_count, block_len)
        .transpose(1, 2, 0, 3)
        .reshape(5, patch_east_count, patch_north_count)
    )
    return (
        potential_warmth_updated,
        saltiness_updated,
        coupled_surface_velocity,
        glacial_patch_update,
    )


def solution(mesh):
    placed = (
        P(None, "grp", "gy"),
        P(None, "grp", "gy"),
        P(None, "grp", "gy"),
        P(None, "grp", "gy"),
        P(None, "grp", "gy"),
        P(None, "grp", "gy"),
        P(None, "grp", "gy"),
        P("grp", "gy"),
        P("grp", "gy"),
        P("grp", "gy"),
    )
    return jax.shard_map(
        per_device,
        mesh=mesh,
        in_specs=placed,
        out_specs=(
            P(None, "grp", "gy"),
            P(None, "grp", "gy"),
            P(None, "grp", "gy"),
            P(None, "grp", "gy"),
        ),
        check_vma=False,
    )
```

profile of v0, /device:TPU:0, one launch (start us, length us, event | category | flops | bytes accessed | tf_op | source)
XLA Modules:
  0.0 56.2 jit_solution(15809073682449732401)
XLA Ops:
  0.7 0.9 %fusion.116 = (f32[16,512]{1,0:T(8,128)S(1)}, f32[1,16,512]{2,1,0:T(8,128)S(1)}) fusion(s32[16,512]{1,0:T(8,128)} %param.19), kind=kLoop, calls=%fused_computation.218 | loop fusion | flops 8192 | bytes 98304 | tf_op jit(solution)/shard_map/convert_element_type | solution.py:197
  1.6 1.5 %pad_maximum_fusion.10 = (f32[49,1,512]{2,1,0:T(1,128)S(1)}, f32[49,1,512]{2,1,0:T(1,128)S(1)}) fusion(f32[1,16,512]{2,1,0:T(8,128)S(1)} %get-tuple-element.60, f32[24,16,512]{2,1,0:T(8,128)} %param.13, f32[24,16,512]{2,1,0:T(8,128)} %param.12), kind=kLoop, calls=%fused_computation.36 | loop fusion | flops 100352 | bytes 1806336 | tf_op jit(solution)/shard_map/slice | solution.py:28
  3.2 0.5 collective-permute-start
  3.7 5.0 %collective-permute-start.1 = (f32[49,1,512]{2,1,0:T(1,128)S(1)}, f32[49,1,512]{2,1,0:T(1,128)S(1)}, u32[]{:S(2)}, u32[]{:S(2)}) collective-permute-start(f32[49,1,512]{2,1,0:T(1,128)S(1)} %get-tuple-element.35), channel_id=1, source_target_pairs={{2,0},{4,2},{6,4},{8,6},{10,8},{12,10},{14,12},{16,14},{18,16},{20... | collective-permute-start | bytes 301064 | tf_op jit(solution)/shard_map/ppermute | solution.py:33
  8.9 2.2 %collective-permute-done = f32[49,1,512]{2,1,0:T(1,128)S(1)} collective-permute-done((f32[49,1,512]{2,1,0:T(1,128)S(1)}, f32[49,1,512]{2,1,0:T(1,128)S(1)}, u32[]{:S(2)}, u32[]{:S(2)}) %collective-permute-start) | collective-permute-done | bytes 100384 | tf_op jit(solution)/shard_map/ppermute | solution.py:31
  11.1 0.4 pad_maximum_fusion.4
  11.5 0.3 copy.26
  11.7 2.0 %collective-permute-start.2 = (f32[49,18,1]{0,2,1:T(1,128)S(1)}, f32[49,18,1]{0,2,1:T(1,128)S(1)}, u32[]{:S(2)}, u32[]{:S(2)}) collective-permute-start(f32[49,18,1]{0,2,1:T(1,128)S(1)} %copy.26), channel_id=1, source_target_pairs={{0,1},{1,0},{2,3},{3,2},{4,5},{5,4},{6,7},{7,6},{8,9},{9,8},{10,11... | collective-permute-start | bytes 10592 | tf_op jit(solution)/shard_map/ppermute | solution.py:31
  13.7 0.3 copy.27
  14.1 1.3 %collective-permute-done.2 = f32[49,18,1]{0,2,1:T(1,128)S(1)} collective-permute-done((f32[49,18,1]{0,2,1:T(1,128)S(1)}, f32[49,18,1]{0,2,1:T(1,128)S(1)}, u32[]{:S(2)}, u32[]{:S(2)}) %collective-permute-start.2) | collective-permute-done | bytes 3560 | tf_op jit(solution)/shard_map/ppermute | solution.py:31
  15.4 0.3 copy.28
  15.8 2.0 %collective-permute-done.3 = f32[49,18,1]{0,2,1:T(1,128)} collective-permute-done((f32[49,18,1]{0,2,1:T(1,128)S(1)}, f32[49,18,1]{0,2,1:T(1,128)}, u32[]{:S(2)}, u32[]{:S(2)}) %collective-permute-start.3) | collective-permute-done | bytes 3560 | tf_op jit(solution)/shard_map/ppermute | solution.py:33
  17.8 1.0 %copy.29 = f32[49,18,1]{2,1,0:T(8,128)S(1)} copy(f32[49,18,1]{0,2,1:T(1,128)} %collective-permute-done.3) | data formatting | bytes 7056 | tf_op jit(solution)/shard_map/ppermute | solution.py:33
  18.8 1.8 %maximum_select_fusion = f32[49,18,514]{2,1,0:T(8,128)S(1)} fusion(f32[49,18,1]{2,1,0:T(8,128)S(1)} %copy.29, f32[49,1,512]{2,1,0:T(1,128)S(1)} %collective-permute-done.1, f32[1,16,512]{2,1,0:T(8,128)S(1)} %get-tuple-element.60, f32[24,16,512]{2,1,0:T(8,128)S(1)} %copy-done.1, f32[24,16,512]{2,1,0:T(8,128)S(1)} %copy-done, ...), kind=kLoop, calls=%fused_computation | loop fusion | flops 3173436 | bytes 3627298 | tf_op jit(solution)/shard_map/jit(_where)/select_n | solution.py:150
  20.6 0.1 slice_multiply_fusion
  20.7 1.7 %fusion.3 = f32[48,16,512]{2,1,0:T(8,128)S(1)} fusion(f32[49,18,514]{2,1,0:T(8,128)S(1)} %maximum_select_fusion, f32[16,512]{1,0:T(8,128)S(1)} %get-tuple-element.55, f32[16,512]{1,0:T(8,128)S(1)} %get-tuple-element.56, f32[16,512]{1,0:T(8,128)S(1)} %get-tuple-element.57, f32[16,512]{1,0:T(8,128)S(1)} %get-tuple-element.58, f32[16,512]{1,0:T(8,128)S(1)} %get-tuple-element.54), kind=kLoop, calls=%fused_computation.5 | loop fusion | flops 5111808 | bytes 9601024 | tf_op jit(solution)/shard_map/add | solution.py:165
  22.5 1.0 %fusion.114 = (f32[24,16,512]{2,1,0:T(8,128)}, f32[24,16,512]{2,1,0:T(8,128)S(1)}) fusion(f32[48,16,512]{2,1,0:T(8,128)S(1)} %fusion.3), kind=kLoop, calls=%fused_computation.216 | loop fusion | bytes 3145728 | tf_op jit(solution)/shard_map/slice | solution.py:252
  23.7 4.4 %collective-permute-start.5 = (f32[12,4,512]{2,1,0:T(4,128)S(1)}, f32[12,4,512]{2,1,0:T(4,128)S(1)}, u32[]{:S(2)}, u32[]{:S(2)}) collective-permute-start(f32[12,4,512]{2,1,0:T(4,128)S(1)} %get-tuple-element.51), channel_id=1, source_target_pairs={{2,0},{4,2},{6,4},{8,6},{10,8},{12,10},{14,12},{16,14},{18,16},{20... | collective-permute-start | bytes 294920 | tf_op jit(solution)/shard_map/ppermute | solution.py:33
  28.1 2.3 %collective-permute-done.4 = f32[12,4,512]{2,1,0:T(4,128)S(1)} collective-permute-done((f32[12,4,512]{2,1,0:T(4,128)S(1)}, f32[12,4,512]{2,1,0:T(4,128)S(1)}, u32[]{:S(2)}, u32[]{:S(2)}) %collective-permute-start.4) | collective-permute-done | bytes 98336 | tf_op jit(solution)/shard_map/ppermute | solution.py:31
  30.4 0.1 pad_maximum_fusion.7
  30.5 0.1 collective-permute-start.6
  30.7 2.0 %collective-permute-start.7 = (f32[12,24,4]{2,1,0:T(8,128)S(1)}, f32[12,24,4]{2,1,0:T(8,128)S(1)}, u32[]{:S(2)}, u32[]{:S(2)}) collective-permute-start(f32[12,24,4]{2,1,0:T(8,128)S(1)} %get-tuple-element.49), channel_id=1, source_target_pairs={{1,0},{0,1},{3,2},{2,3},{5,4},{4,5},{7,6},{6,7},{9,8},{8,9},{11,10... | collective-permute-start | bytes 13832 | tf_op jit(solution)/shard_map/ppermute | solution.py:33
  32.6 3.1 %collective-permute-done.6 = f32[12,24,4]{2,1,0:T(8,128)S(1)} collective-permute-done((f32[12,24,4]{2,1,0:T(8,128)S(1)}, f32[12,24,4]{2,1,0:T(8,128)S(1)}, u32[]{:S(2)}, u32[]{:S(2)}) %collective-permute-start.6) | collective-permute-done | bytes 4640 | tf_op jit(solution)/shard_map/ppermute | solution.py:31
  35.8 1.6 %collective-permute-done.7 = f32[12,24,4]{2,1,0:T(8,128)S(1)} collective-permute-done((f32[12,24,4]{2,1,0:T(8,128)S(1)}, f32[12,24,4]{2,1,0:T(8,128)S(1)}, u32[]{:S(2)}, u32[]{:S(2)}) %collective-permute-start.7) | collective-permute-done | bytes 4640 | tf_op jit(solution)/shard_map/ppermute | solution.py:33
  37.3 0.4 maximum_select_fusion.1
  37.8 0.1 slice_bitcast_fusion.2
  37.9 0.3 copy.30
  38.2 0.3 copy.31
  38.5 0.3 copy.32
  38.8 0.2 stack.39
  39.0 1.2 %maximum_bitcast_fusion = f32[4,1,12,24,136]{4,0,3,2,1:T(4,128)S(1)} fusion(f32[1,12,24,136]{3,0,2,1:T(1,128)S(1)} %stack.39, f32[1,12,24,136]{3,0,2,1:T(1,128)S(1)} %copy.32, f32[1,12,24,136]{3,0,2,1:T(1,128)S(1)} %copy.31, f32[1,12,24,136]{3,0,2,1:T(1,128)S(1)} %copy.30), kind=kLoop, calls=%fused_computation.14 | loop fusion | flops 470016 | bytes 1253376 | tf_op jit(solution)/shard_map/broadcast_in_dim | solution.py:230
  40.3 0.1 slice.484
  40.4 0.1 slice.483
  40.6 0.2 fusion.21
  40.8 0.2 fusion.18
  41.0 0.3 fusion.31
  41.3 0.1 slice.504
  41.5 0.3 fusion.38
  41.8 0.1 slice.503
  41.9 0.2 multiply_multiply_fusion.9
  42.2 0.2 multiply_multiply_fusion.10
  42.4 0.3 fusion.48
  42.7 0.1 slice.519
  42.9 0.3 fusion.55
  43.2 0.1 slice.518
  43.4 0.2 multiply_multiply_fusion.7
  43.7 0.2 multiply_multiply_fusion.5
  43.9 0.3 fusion.65
  44.2 0.1 slice.534
  44.3 0.3 fusion.72
  44.7 0.1 slice.533
  44.8 0.2 multiply_multiply_fusion.4
  45.1 0.2 multiply_multiply_fusion.2
  45.3 0.6 %multiply_multiply_fusion.1 = (f32[4,1,24,136]{3,0,2,1:T(4,128)S(1)}, f32[4,1,24,136]{3,0,2,1:T(4,128)S(1)}, f32[4,1,24,136]{3,0,2,1:T(4,128)S(1)}) fusion(f32[4,1,12,24,136]{4,0,3,2,1:T(4,128)S(1)} %maximum_bitcast_fusion, f32[4,1,24,136]{3,0,2,1:T(4,128)S(1)} %fusion.72, f32[4,1,24,136]{3,0,2,1:T(4,128)S(1)} %fusion.65, ...), kind=kLoop, calls=%fused_computation.146 | loop fusion | flops 665856 | bytes 1095552 | tf_op jit(solution)/shard_map/mul | solution.py:130
  46.0 0.1 bitcast_dynamic-update-slice_fusion
  46.1 0.1 fusion.94
  46.2 0.1 fusion.93
  46.3 0.1 fusion.92
  46.4 1.0 %fusion.10 = f32[2,2,5,16,128]{4,1,3,2,0:T(2,128)} fusion(f32[4,1,5,16,128]{4,0,3,2,1:T(4,128)S(1)} %fusion.92, s32[2,2]{1,0:T(2,128)S(1)} %multiply_add_fusion, s32[4]{0:T(128)S(1)} %bitcast.317), kind=kOutput, calls=%fused_computation.28 | convolution fusion | flops 1966096 | bytes 327712 | tf_op jit(solution)/shard_map/sb,bfxy->sfxy/dot_general | solution.py:235
  47.4 3.4 %all-to-all-start = ((f32[2,2,5,16,128]{4,1,3,2,0:T(2,128)}), f32[2,2,5,16,128]{4,1,3,2,0:T(2,128)S(1)}, u32[]{:S(2)}, u32[]{:S(2)}) async-start(f32[2,2,5,16,128]{4,1,3,2,0:T(2,128)} %fusion.10), calls=%async_computation | async-start | bytes 327680 | tf_op jit(solution)/shard_map/all_to_all | solution.py:238
  50.9 0.1 fusion.96
  51.1 0.6 %add_multiply_fusion = f32[2,16,512]{2,1,0:T(8,128)} fusion(f32[2,16,512]{2,1,0:T(8,128)S(1)} %copy-done.3, f32[2,16,512]{2,1,0:T(8,128)S(1)} %mul.614, f32[16,512]{1,0:T(8,128)S(1)} %get-tuple-element.59), kind=kLoop, calls=%fused_computation.172 | loop fusion | flops 32768 | bytes 229376 | tf_op jit(solution)/shard_map/mul | solution.py:253
  51.7 3.8 %all-to-all-done = f32[2,2,5,16,128]{4,1,3,2,0:T(2,128)S(1)} async-done(((f32[2,2,5,16,128]{4,1,3,2,0:T(2,128)}), f32[2,2,5,16,128]{4,1,3,2,0:T(2,128)S(1)}, u32[]{:S(2)}, u32[]{:S(2)}) %all-to-all-start) | async-done | bytes 163872 | tf_op jit(solution)/shard_map/all_to_all | solution.py:238
  55.5 0.7 %copy.38 = f32[4,5,2,8,128]{4,3,0,2,1:T(8,128)} copy(f32[4,5,2,8,128]{4,3,2,1,0:T(8,128)S(1)} %bitcast.315) | data formatting | bytes 327680 | tf_op jit(solution)/shard_map/reshape | solution.py:257
  (83 shorter events, 0.8 us)
Async XLA Ops:
  0.6 10.4 %copy-start = (f32[24,16,512]{2,1,0:T(8,128)S(1)}, f32[24,16,512]{2,1,0:T(8,128)}, u32[]{:S(2)}) copy-start(f32[24,16,512]{2,1,0:T(8,128)} %param.12) | copy-start | bytes 2359300
  0.6 10.4 %copy-start.1 = (f32[24,16,512]{2,1,0:T(8,128)S(1)}, f32[24,16,512]{2,1,0:T(8,128)}, u32[]{:S(2)}) copy-start(f32[24,16,512]{2,1,0:T(8,128)} %param.13) | copy-start | bytes 2359300
  0.7 8.1 %copy-start.4 = (f32[5,16,512]{2,1,0:T(8,128)S(1)}, f32[5,16,512]{2,1,0:T(8,128)}, u32[]{:S(2)}) copy-start(f32[5,16,512]{2,1,0:T(8,128)} %param.16) | copy-start | bytes 491524
  0.7 8.1 %copy-start.6 = (f32[5,16,512]{2,1,0:T(8,128)S(1)}, f32[5,16,512]{2,1,0:T(8,128)}, u32[]{:S(2)}) copy-start(f32[5,16,512]{2,1,0:T(8,128)} %param.17) | copy-start | bytes 491524
  0.7 8.1 %copy-start.5 = (f32[5,16,512]{2,1,0:T(8,128)S(1)}, f32[5,16,512]{2,1,0:T(8,128)}, u32[]{:S(2)}) copy-start(f32[5,16,512]{2,1,0:T(8,128)} %param.18) | copy-start | bytes 491524
  0.7 8.1 %copy-start.3 = (f32[2,16,512]{2,1,0:T(8,128)S(1)}, f32[2,16,512]{2,1,0:T(8,128)}, u32[]{:S(2)}) copy-start(f32[2,16,512]{2,1,0:T(8,128)} %param.14) | copy-start | bytes 196612
  0.7 8.2 %copy-start.8 = (f32[2,16,512]{2,1,0:T(8,128)S(1)}, f32[2,16,512]{2,1,0:T(8,128)}, u32[]{:S(2)}) copy-start(f32[2,16,512]{2,1,0:T(8,128)} %param.15) | copy-start | bytes 196612
  3.2 7.9 %collective-permute-start = (f32[49,1,512]{2,1,0:T(1,128)S(1)}, f32[49,1,512]{2,1,0:T(1,128)S(1)}, u32[]{:S(2)}, u32[]{:S(2)}) collective-permute-start(f32[49,1,512]{2,1,0:T(1,128)S(1)} %get-tuple-element.34), channel_id=1, source_target_pairs={{0,2},{2,4},{4,6},{6,8},{8,10},{10,12},{12,14},{14,16},{16,18},{18... | collective-permute-start | bytes 301064 | tf_op jit(solution)/shard_map/ppermute | solution.py:31
  3.7 7.4 %collective-permute-start.1 = (f32[49,1,512]{2,1,0:T(1,128)S(1)}, f32[49,1,512]{2,1,0:T(1,128)S(1)}, u32[]{:S(2)}, u32[]{:S(2)}) collective-permute-start(f32[49,1,512]{2,1,0:T(1,128)S(1)} %get-tuple-element.35), channel_id=1, source_target_pairs={{2,0},{4,2},{6,4},{8,6},{10,8},{12,10},{14,12},{16,14},{18,16},{20... | collective-permute-start | bytes 301064 | tf_op jit(solution)/shard_map/ppermute | solution.py:33
  11.7 3.7 %collective-permute-start.2 = (f32[49,18,1]{0,2,1:T(1,128)S(1)}, f32[49,18,1]{0,2,1:T(1,128)S(1)}, u32[]{:S(2)}, u32[]{:S(2)}) collective-permute-start(f32[49,18,1]{0,2,1:T(1,128)S(1)} %copy.26), channel_id=1, source_target_pairs={{0,1},{1,0},{2,3},{3,2},{4,5},{5,4},{6,7},{7,6},{8,9},{9,8},{10,11... | collective-permute-start | bytes 10592 | tf_op jit(solution)/shard_map/ppermute | solution.py:31
  14.0 3.8 %collective-permute-start.3 = (f32[49,18,1]{0,2,1:T(1,128)S(1)}, f32[49,18,1]{0,2,1:T(1,128)}, u32[]{:S(2)}, u32[]{:S(2)}) collective-permute-start(f32[49,18,1]{0,2,1:T(1,128)S(1)} %copy.27), channel_id=1, source_target_pairs={{1,0},{0,1},{3,2},{2,3},{5,4},{4,5},{7,6},{6,7},{9,8},{8,9},{11,10... | collective-permute-start | bytes 10592 | tf_op jit(solution)/shard_map/ppermute | solution.py:33
  22.5 1.1 %copy-start.7 = (s32[16,512]{1,0:T(8,128)S(1)}, s32[16,512]{1,0:T(8,128)}, u32[]{:S(2)}) copy-start(s32[16,512]{1,0:T(8,128)} %param.19) | copy-start | bytes 98308
  22.5 1.1 %copy-start.9 = (s32[16,512]{1,0:T(8,128)S(1)}, s32[16,512]{1,0:T(8,128)}, u32[]{:S(2)}) copy-start(s32[16,512]{1,0:T(8,128)} %param.20) | copy-start | bytes 98308
  23.6 14.3 %copy-start.2 = (f32[24,16,512]{2,1,0:T(8,128)}, f32[24,16,512]{2,1,0:T(8,128)S(1)}, u32[]{:S(2)}) copy-start(f32[24,16,512]{2,1,0:T(8,128)S(1)} %get-tuple-element.62) | copy-start | bytes 2359300
  23.6 6.8 %collective-permute-start.4 = (f32[12,4,512]{2,1,0:T(4,128)S(1)}, f32[12,4,512]{2,1,0:T(4,128)S(1)}, u32[]{:S(2)}, u32[]{:S(2)}) collective-permute-start(f32[12,4,512]{2,1,0:T(4,128)S(1)} %get-tuple-element.50), channel_id=1, source_target_pairs={{0,2},{2,4},{4,6},{6,8},{8,10},{10,12},{12,14},{14,16},{16,18},{18... | collective-permute-start | bytes 294920 | tf_op jit(solution)/shard_map/ppermute | solution.py:31
  23.7 6.7 %collective-permute-start.5 = (f32[12,4,512]{2,1,0:T(4,128)S(1)}, f32[12,4,512]{2,1,0:T(4,128)S(1)}, u32[]{:S(2)}, u32[]{:S(2)}) collective-permute-start(f32[12,4,512]{2,1,0:T(4,128)S(1)} %get-tuple-element.51), channel_id=1, source_target_pairs={{2,0},{4,2},{6,4},{8,6},{10,8},{12,10},{14,12},{16,14},{18,16},{20... | collective-permute-start | bytes 294920 | tf_op jit(solution)/shard_map/ppermute | solution.py:33
  30.5 5.2 %collective-permute-start.6 = (f32[12,24,4]{2,1,0:T(8,128)S(1)}, f32[12,24,4]{2,1,0:T(8,128)S(1)}, u32[]{:S(2)}, u32[]{:S(2)}) collective-permute-start(f32[12,24,4]{2,1,0:T(8,128)S(1)} %get-tuple-element.48), channel_id=1, source_target_pairs={{0,1},{1,0},{2,3},{3,2},{4,5},{5,4},{6,7},{7,6},{8,9},{9,8},{10,11... | collective-permute-start | bytes 13832 | tf_op jit(solution)/shard_map/ppermute | solution.py:31
  30.7 6.7 %collective-permute-start.7 = (f32[12,24,4]{2,1,0:T(8,128)S(1)}, f32[12,24,4]{2,1,0:T(8,128)S(1)}, u32[]{:S(2)}, u32[]{:S(2)}) collective-permute-start(f32[12,24,4]{2,1,0:T(8,128)S(1)} %get-tuple-element.49), channel_id=1, source_target_pairs={{1,0},{0,1},{3,2},{2,3},{5,4},{4,5},{7,6},{6,7},{9,8},{8,9},{11,10... | collective-permute-start | bytes 13832 | tf_op jit(solution)/shard_map/ppermute | solution.py:33
  45.1 1.3 %copy-start.10 = (s32[1,4]{1,0:T(1,128)S(1)}, s32[1,4]{1,0:T(1,128)}, u32[]{:S(2)}) copy-start(s32[1,4]{1,0:T(1,128)} %param.21) | copy-start | bytes 52
  47.4 8.1 %all-to-all-start = ((f32[2,2,5,16,128]{4,1,3,2,0:T(2,128)}), f32[2,2,5,16,128]{4,1,3,2,0:T(2,128)S(1)}, u32[]{:S(2)}, u32[]{:S(2)}) async-start(f32[2,2,5,16,128]{4,1,3,2,0:T(2,128)} %fusion.10), calls=%async_computation | async-start | bytes 327680 | tf_op jit(solution)/shard_map/all_to_all | solution.py:238
where the time goes:
time: 56.5 us; the launch traced here: 56.2 us
  starting transfers between devices  17.7 us (31%)
  waiting for transfers between devices  16.3 us (29%)
  other arithmetic  13.2 us (23%)
  local copies, waits for them, and re-layouts  6.55 us (12%)
  between operations  1.4 us (2%)
  matrix products  1.04 us (2%)
    ppermute x4, starting transfers between devices, extended(): lax.ppermute(head, axis, [((i + 1) % count, i) for i in range(count)])  11.5 us
    ppermute x4, waiting for transfers between devices, extended(): lax.ppermute(tail, axis, [(i, (i + 1) % count) for i in range(count)])  8.9 us
    all_to_all x1, waiting for transfers between devices, per_device(): lax.all_to_all(picked.reshape((groups, pair_count) + picked.shape[1:]), '...  3.77 us
    ppermute x4, waiting for transfers between devices, extended(): lax.ppermute(head, axis, [((i + 1) % count, i) for i in range(count)])  3.62 us
    all_to_all x1, starting transfers between devices, per_device(): lax.all_to_all(picked.reshape((groups, pair_count) + picked.shape[1:]), '...  3.43 us
    ppermute x4, starting transfers between devices, extended(): lax.ppermute(tail, axis, [(i, (i + 1) % count) for i in range(count)])  2.73 us
    select_n x2, other arithmetic, close_rims(): return jnp.where(low_rim | high_rim, 0.0, padded)  2.19 us
    slice x3, other arithmetic, extended(): lax.slice_in_dim(cells, cells.shape[dim] - width, cells.shape[dim], axis=...  2.02 us
  transfers between devices with their start and end apart: 9, of which 7 were waited for; matrix products, arithmetic and copies ran while one was open for 3% of the time, Pallas kernels for 0%

commit v1 on v0

v1 whole, which is shorter than its diff:
```python
import functools

import jax
import jax.numpy as jnp
from jax import lax
from jax.experimental import pallas as pl
from jax.experimental.pallas import tpu as pltpu
from jax.sharding import PartitionSpec as P

NSUB = 4
DIFFUSIVITY = 0.2
STRENGTH_COEF = 20.0
MIN_MASS = 0.5
RELAX_RATE = 0.5
ECCENTRIC = 4.0
DELTA_FLOOR = 0.0025
SPEED_FLOOR = 0.01
CORIOLIS = 0.5
HEAT_COEF = 4.0
THIN_LIMIT = 0.1
FREEZING = -1.8
WARMTH_FACTOR = 0.05
STRESS_SCALE = 0.5

LANES = 128
PLANES = 12
A_PLANE, H_PLANE, ICY_PLANE = 9, 10, 11


def shift(field, offset, axis):
    size = field.shape[axis]
    return pltpu.roll(field, (-offset) % size, axis)


def kernel(
    n_grp, n_gy, levels, rows, cols, nblock,
    home, pw, sa, sv, af, gvs, cc, ct, si, di,
    pw_out, sa_out, vel_out, glac_out,
    win, ccv, ctv, siv, div_, pwv, sav, pwo, sao, coef, cvel, heat,
    icy_rows, wet_rows, halo_rows,
    pack_hi, pack_lo, tpack_hi, tpack_lo, got_hi, got_lo, tgot_hi, tgot_lo,
    mine, picks,
    in_sem, out_sem, row_send, row_recv, col_send, col_recv, patch_send, patch_recv,
):
    g = lax.axis_index("grp")
    y = lax.axis_index("gy")
    east = lax.rem(g + 1, n_grp)
    west = lax.rem(g + n_grp - 1, n_grp)
    has_up = y < n_gy - 1
    has_dn = y > 0
    ext = rows + 2 * NSUB
    block_len = cols // nblock
    pair = nblock // n_gy

    center = (slice(0, rows), slice(0, cols))
    loads = [
        pltpu.make_async_copy(src, dst, in_sem.at[i])
        for i, (src, dst) in enumerate(
            (
                (cc, ccv),
                (ct, ctv),
                (di, div_),
                (si, siv),
                (gvs, win.at[0:5, 0:rows, 0:cols]),
                (sv, win.at[5:7, 0:rows, 0:cols]),
                (af, win.at[7:9, 0:rows, 0:cols]),
                (pw, pwv),
                (sa, sav),
            )
        )
    ]
    for load in loads:
        load.start()

    barrier = pltpu.get_barrier_semaphore()

    def greet(gg, yy):
        pl.semaphore_signal(
            barrier, inc=1, device_id={"grp": gg, "gy": yy},
            device_id_type=pl.DeviceIdType.MESH,
        )

    greet(east, y)
    greet(west, y)
    for k in range(1, n_gy):
        greet(g, lax.rem(y + k, n_gy))

    @pl.when(has_up)
    def _():
        greet(east, y + 1)
        greet(west, y + 1)

    @pl.when(has_dn)
    def _():
        greet(east, y - 1)
        greet(west, y - 1)

    both = jnp.where(has_up, 2, 0) + jnp.where(has_dn, 2, 0)

    for load in loads[:4]:
        load.wait()
    win[A_PLANE, 0:rows, 0:cols] = jnp.sum(ccv[...], axis=0)
    win[H_PLANE, 0:rows, 0:cols] = jnp.sum(ctv[...], axis=0)
    win[ICY_PLANE, 0:rows, 0:cols] = div_[...].astype(jnp.float32)
    wet = siv[...].astype(jnp.float32)
    for load in loads[4:7]:
        load.wait()

    lane16 = lax.broadcasted_iota(jnp.int32, (rows, LANES), 1)

    def pack(entries):
        out = jnp.zeros((rows, LANES), jnp.float32)
        for tile, first, place, width in entries:
            moved = pltpu.roll(tile, (place - first) % LANES, 1)
            out = jnp.where((lane16 >= place) & (lane16 < place + width), moved, out)
        return out

    wet_lane = PLANES * NSUB
    hi = slice(cols - LANES, cols)
    lo = slice(0, LANES)
    pack_hi[...] = pack(
        [(win[p, 0:rows, hi], LANES - NSUB, NSUB * p, NSUB) for p in range(PLANES)]
        + [(wet[:, hi], LANES - 1, wet_lane, 1)]
    )
    pack_lo[...] = pack(
        [(win[p, 0:rows, lo], 0, NSUB * p, NSUB) for p in range(PLANES)]
        + [(wet[:, lo], 0, wet_lane, 1)]
    )

    pl.semaphore_wait(barrier, 1 + n_gy + both)

    def remote(src, dst, send, recv, gg, yy):
        return pltpu.make_async_remote_copy(
            src_ref=src, dst_ref=dst, send_sem=send, recv_sem=recv,
            device_id={"grp": gg, "gy": yy}, device_id_type=pl.DeviceIdType.MESH,
        )

    count = 0
    ice_rows, tracer_rows = [], []
    for to, first, at, edge, sub in (
        (west, 0, rows, 0, 7),
        (east, rows - NSUB, rows + NSUB, rows - 1, 0),
    ):
        src_rows = slice(first, first + NSUB)
        dst_rows = slice(at, at + NSUB)
        ice_pairs = (
            (gvs.at[:, src_rows, :], win.at[0:5, dst_rows, 0:cols]),
            (sv.at[:, src_rows, :], win.at[5:7, dst_rows, 0:cols]),
            (af.at[:, src_rows, :], win.at[7:9, dst_rows, 0:cols]),
            (win.at[A_PLANE : H_PLANE + 1, src_rows, 0:cols],
             win.at[A_PLANE : H_PLANE + 1, dst_rows, 0:cols]),
            (di.at[src_rows, :], icy_rows.at[at - rows : at - rows + NSUB, :]),
        )
        tracer_pairs = (
            (si.at[edge : edge + 1, :], wet_rows.at[sub : sub + 1, :]),
            (pw.at[:, edge : edge + 1, :], halo_rows.at[0:levels, sub : sub + 1, :]),
            (sa.at[:, edge : edge + 1, :], halo_rows.at[levels : 2 * levels, sub : sub + 1, :]),
        )
        for pairs, keep in ((ice_pairs, ice_rows), (tracer_pairs, tracer_rows)):
            for src, dst in pairs:
                keep.append(remote(src, dst, row_send.at[count], row_recv.at[count], to, y))
                count += 1
    for copy in ice_rows:
        copy.start()

    ice_up = [
        remote(pack_hi, got_lo.at[0:rows, :], col_send.at[0], col_recv.at[0], g, y + 1),
        remote(pack_hi.at[0:NSUB, :], got_lo.at[rows : rows + NSUB, :],
               col_send.at[1], col_recv.at[1], west, y + 1),
        remote(pack_hi.at[rows - NSUB : rows, :], got_lo.at[rows + NSUB : ext, :],
               col_send.at[2], col_recv.at[2], east, y + 1),
    ]
    ice_dn = [
        remote(pack_lo, got_hi.at[0:rows, :], col_send.at[3], col_recv.at[3], g, y - 1),
        remote(pack_lo.at[0:NSUB, :], got_hi.at[rows : rows + NSUB, :],
               col_send.at[4], col_recv.at[4], west, y - 1),
        remote(pack_lo.at[rows - NSUB : rows, :], got_hi.at[rows + NSUB : ext, :],
               col_send.at[5], col_recv.at[5], east, y - 1),
    ]
    tr_up = remote(tpack_hi, tgot_lo, col_send.at[6], col_recv.at[6], g, y + 1)
    tr_dn = remote(tpack_lo, tgot_hi, col_send.at[7], col_recv.at[7], g, y - 1)

    @pl.when(has_up)
    def _():
        for copy in ice_up:
            copy.start()

    @pl.when(has_dn)
    def _():
        for copy in ice_dn:
            copy.start()

    for copy in tracer_rows:
        copy.start()

    for load in loads[7:]:
        load.wait()
    for out, cut, first in ((tpack_hi, hi, LANES - 1), (tpack_lo, lo, 0)):
        out[...] = pack(
            [(pwv[l, :, cut], first, l, 1) for l in range(levels)]
            + [(sav[l, :, cut], first, levels + l, 1) for l in range(levels)]
        )

    @pl.when(has_up)
    def _():
        tr_up.start()

    @pl.when(has_dn)
    def _():
        tr_dn.start()

    coverage = ccv[...]
    per_cat = HEAT_COEF * coverage * coverage / (ctv[...] + THIN_LIMIT * coverage)
    heat[...] = (
        (WARMTH_FACTOR * wet)
        * (win[ICY_PLANE, 0:rows, 0:cols] * (pwv[0] - FREEZING) * jnp.sum(per_cat, axis=0))
    )

    @pl.when(jnp.logical_not(has_up))
    def _():
        got_hi[...] = jnp.zeros_like(got_hi)
        tgot_hi[...] = jnp.zeros_like(tgot_hi)

    @pl.when(jnp.logical_not(has_dn))
    def _():
        got_lo[...] = jnp.zeros_like(got_lo)
        tgot_lo[...] = jnp.zeros_like(tgot_lo)

    for copy in ice_rows:
        copy.wait_recv()

    @pl.when(has_up)
    def _():
        for copy in ice_dn:
            copy.wait_recv()

    @pl.when(has_dn)
    def _():
        for copy in ice_up:
            copy.wait_recv()

    win[ICY_PLANE, rows:ext, 0:cols] = icy_rows[...].astype(jnp.float32)
    lane24 = lax.broadcasted_iota(jnp.int32, (ext, LANES), 1)
    from_hi, from_lo = got_hi[...], got_lo[...]
    for p in range(PLANES):
        high = pltpu.roll(from_hi, (-NSUB * p) % LANES, 1)
        low = pltpu.roll(from_lo, (LANES - NSUB - NSUB * p) % LANES, 1)
        win[p, :, cols : cols + LANES] = jnp.where(
            lane24 < NSUB, high, jnp.where(lane24 >= LANES - NSUB, low, 0.0)
        )

    vel_u, vel_v = win[0], win[1]
    sig_one, sig_two, sig_shear = win[2], win[3], win[4]
    cur_u, cur_v, wind_u, wind_v = win[5], win[6], win[7], win[8]
    conc, thick, icy = win[A_PLANE], win[H_PLANE], win[ICY_PLANE]
    strength = thick * jnp.exp(-STRENGTH_COEF * (1.0 - conc))
    mass = thick + MIN_MASS
    keep = icy * (1.0 / (1.0 + RELAX_RATE))
    push = keep * strength * RELAX_RATE
    push_dev = push * (1.0 / ECCENTRIC)

    def drag(u, v):
        square = (cur_u - u) ** 2 + (cur_v - v) ** 2 + SPEED_FLOOR
        return conc * (square * lax.rsqrt(square))

    for _ in range(NSUB):
        u_east = shift(vel_u, 1, 0) - vel_u
        v_north = shift(vel_v, 1, 1) - vel_v
        u_north = shift(vel_u, 1, 1) - vel_u
        v_east = shift(vel_v, 1, 0) - vel_v
        diverge = u_east + v_north
        tension = u_east - v_north
        shear = u_north + v_east
        inverse = lax.rsqrt(
            diverge * diverge
            + (tension * tension + shear * shear) * (1.0 / ECCENTRIC)
            + DELTA_FLOOR
        )
        sig_one = keep * sig_one + push * (diverge * inverse - 1.0)
        scaled = push_dev * inverse
        sig_two = keep * sig_two + scaled * tension
        sig_shear = keep * sig_shear + scaled * shear
        total = sig_one + sig_two
        differ = sig_one - sig_two
        force_u = 0.5 * (total - shift(total, -1, 0)) + (sig_shear - shift(sig_shear, -1, 1))
        force_v = 0.5 * (differ - shift(differ, -1, 1)) + (sig_shear - shift(sig_shear, -1, 0))
        water = drag(vel_u, vel_v)
        scale = icy / (mass + water)
        turn_u = (CORIOLIS * mass) * vel_v
        turn_v = (CORIOLIS * mass) * vel_u
        new_u = (mass * vel_u + force_u + wind_u + water * cur_u + turn_u) * scale
        new_v = (mass * vel_v + force_v + wind_v + water * cur_v - turn_v) * scale
        vel_u, vel_v = new_u, new_v

    state = [f[0:rows, 0:cols] for f in (vel_u, vel_v, sig_one, sig_two, sig_shear)]

    homes = [home[0, b] for b in range(nblock)]

    def choose(slot, field):
        out = jnp.zeros((rows, block_len), jnp.float32)
        for b in range(nblock):
            out = jnp.where(homes[b] == slot, field[:, b * block_len : (b + 1) * block_len], out)
        return out

    span = pair * block_len
    place = pl.ds(pl.multiple_of(y * span, LANES), span)
    patches = []
    for k in range(1, n_gy):
        peer = lax.rem(y + k, n_gy)
        for f in range(5):
            for p in range(pair):
                picks[k - 1, f, :, p * block_len : (p + 1) * block_len] = choose(
                    peer * pair + p, state[f]
                )
        copy = remote(
            picks.at[k - 1], glac_out.at[:, :, place],
            patch_send.at[k - 1], patch_recv.at[k - 1], g, peer,
        )
        copy.start()
        patches.append(copy)
    for f in range(5):
        for p in range(pair):
            mine[f, :, p * block_len : (p + 1) * block_len] = choose(y * pair + p, state[f])
    outs = [pltpu.make_async_copy(mine, glac_out.at[:, :, place], out_sem.at[0])]
    outs[0].start()

    wide_u = icy * drag(vel_u, vel_v)
    tau_u = (wide_u * (vel_u - cur_u))[0:rows, 0:cols]
    tau_v = (wide_u * (vel_v - cur_v))[0:rows, 0:cols]
    cvel[0] = wet * (cur_u[0:rows, 0:cols] + STRESS_SCALE * tau_u)
    cvel[1] = wet * (cur_v[0:rows, 0:cols] + STRESS_SCALE * tau_v)
    outs.append(pltpu.make_async_copy(cvel, vel_out, out_sem.at[1]))
    outs[1].start()

    for copy in tracer_rows:
        copy.wait_recv()

    @pl.when(has_up)
    def _():
        tr_dn.wait_recv()

    @pl.when(has_dn)
    def _():
        tr_up.wait_recv()

    row = lax.broadcasted_iota(jnp.int32, (rows, cols), 0)
    lane = lax.broadcasted_iota(jnp.int32, (rows, cols), 1)
    reps = cols // LANES

    def neighbours(field, edge_rows, high, low):
        edge = jnp.concatenate([edge_rows] * (rows // 8), axis=0)
        high = jnp.concatenate([high] * reps, axis=1)
        low = jnp.concatenate([low] * reps, axis=1)
        return (
            jnp.where(row == rows - 1, edge, shift(field, 1, 0)),
            jnp.where(row == 0, edge, shift(field, -1, 0)),
            jnp.where(lane == cols - 1, high, shift(field, 1, 1)),
            jnp.where(lane == 0, low, shift(field, -1, 1)),
        )

    near = neighbours(
        wet,
        wet_rows[...].astype(jnp.float32),
        pltpu.roll(got_hi[0:rows, :], (LANES - 1 - wet_lane) % LANES, 1),
        pltpu.roll(got_lo[0:rows, :], (-wet_lane) % LANES, 1),
    )
    rate = DIFFUSIVITY * wet
    weights = [rate * n for n in near]
    for i in range(4):
        coef[i] = weights[i]
    coef[4] = 1.0 - (weights[0] + weights[1] + weights[2] + weights[3])

    chunks = 4
    step = levels // chunks
    thi, tlo = tgot_hi[...], tgot_lo[...]
    sem = 2
    for c in range(chunks):
        for src, dst, base in ((pwv, pwo, 0), (sav, sao, levels)):
            for l in range(c * step, (c + 1) * step):
                at = base + l
                field = src[l]
                sides = neighbours(
                    field,
                    halo_rows[at],
                    pltpu.roll(thi, (LANES - 1 - at) % LANES, 1),
                    pltpu.roll(tlo, (-at) % LANES, 1),
                )
                mixed = coef[4] * field
                for i in range(4):
                    mixed = mixed + coef[i] * sides[i]
                if at == 0:
                    mixed = mixed - heat[...]
                dst[l] = mixed
        for src, dst in ((pwo, pw_out), (sao, sa_out)):
            cut = slice(c * step, (c + 1) * step)
            copy = pltpu.make_async_copy(src.at[cut], dst.at[cut], out_sem.at[sem])
            copy.start()
            outs.append(copy)
            sem += 1

    for copy in ice_rows + tracer_rows:
        copy.wait_send()

    @pl.when(has_up)
    def _():
        for copy in ice_up + [tr_up]:
            copy.wait_send()

    @pl.when(has_dn)
    def _():
        for copy in ice_dn + [tr_dn]:
            copy.wait_send()

    for copy in patches:
        copy.wait()
    for copy in outs:
        copy.wait()


def per_device(
    n_grp, n_gy, pw, sa, sv, af, gvs, cc, ct, si, di, home
):
    levels, rows, cols = pw.shape
    nblock = home.shape[1]
    block_len = cols // nblock
    pair = nblock // n_gy
    ext = rows + 2 * NSUB
    f32, i32 = jnp.float32, jnp.int32
    any_space = pl.BlockSpec(memory_space=pl.ANY)
    tile = lambda *shape: pltpu.VMEM(shape, f32)
    return pl.pallas_call(
        functools.partial(kernel, n_grp, n_gy, levels, rows, cols, nblock),
        out_shape=(
            jax.ShapeDtypeStruct(pw.shape, f32),
            jax.ShapeDtypeStruct(sa.shape, f32),
            jax.ShapeDtypeStruct(sv.shape, f32),
            jax.ShapeDtypeStruct(gvs.shape, f32),
        ),
        in_specs=[pl.BlockSpec(memory_space=pltpu.SMEM)] + [any_space] * 9,
        out_specs=(any_space,) * 4,
        scratch_shapes=[
            tile(PLANES, ext, cols + LANES),
            tile(*cc.shape),
            tile(*ct.shape),
            pltpu.VMEM((rows, cols), i32),
            pltpu.VMEM((rows, cols), i32),
            tile(*pw.shape),
            tile(*sa.shape),
            tile(*pw.shape),
            tile(*sa.shape),
            tile(5, rows, cols),
            tile(2, rows, cols),
            tile(rows, cols),
            pltpu.VMEM((2 * NSUB, cols), i32),
            pltpu.VMEM((8, cols), i32),
            tile(2 * levels, 8, cols),
            tile(rows, LANES),
            tile(rows, LANES),
            tile(rows, LANES),
            tile(rows, LANES),
            tile(ext, LANES),
            tile(ext, LANES),
            tile(rows, LANES),
            tile(rows, LANES),
            tile(5, rows, pair * block_len),
            tile(max(n_gy - 1, 1), 5, rows, pair * block_len),
            pltpu.SemaphoreType.DMA((9,)),
            pltpu.SemaphoreType.DMA((10,)),
            pltpu.SemaphoreType.DMA((16,)),
            pltpu.SemaphoreType.DMA((16,)),
            pltpu.SemaphoreType.DMA((8,)),
            pltpu.SemaphoreType.DMA((8,)),
            pltpu.SemaphoreType.DMA((max(n_gy - 1, 1),)),
            pltpu.SemaphoreType.DMA((max(n_gy - 1, 1),)),
        ],
        compiler_params=pltpu.CompilerParams(collective_id=0, has_side_effects=True),
    )(home, pw, sa, sv, af, gvs, cc, ct, si, di)


def solution(mesh):
    field = P(None, "grp", "gy")
    flat = P("grp", "gy")
    return jax.shard_map(
        functools.partial(per_device, mesh.shape["grp"], mesh.shape["gy"]),
        mesh=mesh,
        in_specs=(field,) * 7 + (flat,) * 3,
        out_specs=(field,) * 4,
        check_vma=False,
    )
```

time: 56.5 us -> 21.3 us (0.38)
  starting transfers between devices: 17.7 us -> 0 us
  waiting for transfers between devices: 16.3 us -> 0 us
  Pallas kernels: 0 us -> 16.1 us
  other arithmetic: 13.2 us -> 0 us
  local copies, waits for them, and re-layouts: 6.55 us -> 4.35 us
  matrix products: 1.04 us -> 0 us
  between operations: 1.4 us -> 0.66 us
    pallas_call x0 -> x1, Pallas kernels: none -> 16.1 us  [per_device(): pl.pallas_call(functools.partial(kernel, n_grp, n_gy, levels, rows, cols,...]
    ppermute x8 -> x0, starting transfers between devices: 14.2 us -> none  [the longest x4 11.5 us: extended(): lax.ppermute(head, axis, [((i + 1) % count, i) for i in range(count)])]
    ppermute x8 -> x0, waiting for transfers between devices: 12.5 us -> none  [the longest x4 8.9 us: extended(): lax.ppermute(tail, axis, [(i, (i + 1) % count) for i in range(count)])]
    unnamed x31 -> x10, local copies, waits for them, and re-layouts: 0.45 us -> 4.35 us
    all_to_all x1 -> x0, waiting for transfers between devices: 3.77 us -> none  [per_device(): lax.all_to_all(picked.reshape((groups, pair_count) + picked.shape[1:]), '...]
    div x14 -> x0, other arithmetic: 3.57 us -> none  [the longest x3 0.99 us: evp_subcycles(): glacial_indicator * (ice_mass * vel_v + force_v + wind_v + water_coef * c...]
    all_to_all x1 -> x0, starting transfers between devices: 3.43 us -> none  [per_device(): lax.all_to_all(picked.reshape((groups, pair_count) + picked.shape[1:]), '...]
    slice x52 -> x0, local copies, waits for them, and re-layouts: 2.67 us -> none  [the longest x1 1.04 us: per_device(): smoothed_field[vertical_count_value:2 * vertical_count_value]]
  transfers between devices with their start and end apart: 9 -> 0, of which waited for: 7 -> 0; matrix products, arithmetic and copies ran while one was open for 3% -> 0% of each run, Pallas kernels for 0% -> 0%
where the time goes in v1:
time: 21.3 us; the launch traced here: 21.1 us
  Pallas kernels  16.1 us (76%)
  local copies, waits for them, and re-layouts  4.35 us (20%)
  between operations  0.66 us (3%)
    pallas_call x1, Pallas kernels, per_device(): pl.pallas_call(functools.partial(kernel, n_grp, n_gy, levels, rows, cols,...  16.1 us
    unnamed x10, local copies, waits for them, and re-layouts  4.35 us

profile of v1, /device:TPU:0, one launch (start us, length us, event | category | flops | bytes accessed | tf_op | source)
XLA Modules:
  0.0 21.1 jit_solution(15414844838401257460)
XLA Ops:
  0.6 16.1 %shard_map.129 = (f32[24,16,512]{2,1,0:T(8,128)}, f32[24,16,512]{2,1,0:T(8,128)}, f32[2,16,512]{2,1,0:T(8,128)}, f32[5,16,512]{2,1,0:T(8,128)}) custom-call(s32[1,4]{1,0:T(1,128)} %home.1, f32[24,16,512]{2,1,0:T(8,128)} %pw.1, f32[24,16,512]{2,1,0:T(8,128)} %sa.1, f32[2,16,512]{2,1,0:T(8,128)} %sv.1, f32[2,16,512]{2,1,0:T(8,128)} %af.1, f32[5,16,512]{2,1,0:T(8,128)} %gvs.1, ...), custom_call_target="tpu_custom_call" | custom-call | tf_op jit(solution)/shard_map/pallas_call | solution.py:431
  16.7 0.0 copy-start
  16.7 2.2 %copy.18 = f32[24,16,512]{2,1,0:T(8,128)} copy(f32[24,16,512]{2,1,0:T(8,128)} %get-tuple-element.8) | data formatting | bytes 1572864
  18.9 0.0 copy-done
  18.9 0.0 copy-start.2
  18.9 0.0 copy-start.1
  18.9 0.9 %copy.19 = f32[24,16,512]{2,1,0:T(8,128)} copy(f32[24,16,512]{2,1,0:T(8,128)S(1)} %copy-done) | data formatting | bytes 1572864
  19.8 0.0 copy-done.2
  19.8 0.6 %copy.20 = f32[2,16,512]{2,1,0:T(8,128)} copy(f32[2,16,512]{2,1,0:T(8,128)S(1)} %copy-done.2) | data formatting | bytes 131072
  20.4 0.0 copy-done.1
  20.4 0.7 %copy.21 = f32[5,16,512]{2,1,0:T(8,128)} copy(f32[5,16,512]{2,1,0:T(8,128)S(1)} %copy-done.1) | data formatting | bytes 327680
Async XLA Ops:
  16.7 2.2 %copy-start = (f32[24,16,512]{2,1,0:T(8,128)S(1)}, f32[24,16,512]{2,1,0:T(8,128)}, u32[]{:S(2)}) copy-start(f32[24,16,512]{2,1,0:T(8,128)} %get-tuple-element.9) | copy-start | bytes 2359300
  18.9 0.9 %copy-start.2 = (f32[2,16,512]{2,1,0:T(8,128)S(1)}, f32[2,16,512]{2,1,0:T(8,128)}, u32[]{:S(2)}) copy-start(f32[2,16,512]{2,1,0:T(8,128)} %get-tuple-element.10) | copy-start | bytes 196612
  18.9 1.5 %copy-start.1 = (f32[5,16,512]{2,1,0:T(8,128)S(1)}, f32[5,16,512]{2,1,0:T(8,128)}, u32[]{:S(2)}) copy-start(f32[5,16,512]{2,1,0:T(8,128)} %get-tuple-element.11) | copy-start | bytes 491524

commit v2 on v1

--- a/solution.py
+++ b/solution.py
@@ -35,12 +35,12 @@
 def kernel(
     n_grp, n_gy, levels, rows, cols, nblock,
     home, pw, sa, sv, af, gvs, cc, ct, si, di,
-    pw_out, sa_out, vel_out, glac_out,
-    win, ccv, ctv, siv, div_, pwv, sav, pwo, sao, coef, cvel, heat,
+    pwo, sao, cvel, glac_out,
+    win, ccv, ctv, siv, div_, pwv, sav, coef, heat,
     icy_rows, wet_rows, halo_rows,
     pack_hi, pack_lo, tpack_hi, tpack_lo, got_hi, got_lo, tgot_hi, tgot_lo,
-    mine, picks,
-    in_sem, out_sem, row_send, row_recv, col_send, col_recv, patch_send, patch_recv,
+    picks,
+    in_sem, row_send, row_recv, col_send, col_recv, patch_send, patch_recv,
 ):
     g = lax.axis_index("grp")
     y = lax.axis_index("gy")
@@ -320,17 +320,15 @@
         patches.append(copy)
     for f in range(5):
         for p in range(pair):
-            mine[f, :, p * block_len : (p + 1) * block_len] = choose(y * pair + p, state[f])
-    outs = [pltpu.make_async_copy(mine, glac_out.at[:, :, place], out_sem.at[0])]
-    outs[0].start()
+            glac_out[f, :, pl.ds(pl.multiple_of(y * span + p * block_len, LANES), block_len)] = (
+                choose(y * pair + p, state[f])
+            )
 
     wide_u = icy * drag(vel_u, vel_v)
     tau_u = (wide_u * (vel_u - cur_u))[0:rows, 0:cols]
     tau_v = (wide_u * (vel_v - cur_v))[0:rows, 0:cols]
     cvel[0] = wet * (cur_u[0:rows, 0:cols] + STRESS_SCALE * tau_u)
     cvel[1] = wet * (cur_v[0:rows, 0:cols] + STRESS_SCALE * tau_v)
-    outs.append(pltpu.make_async_copy(cvel, vel_out, out_sem.at[1]))
-    outs[1].start()
 
     for copy in tracer_rows:
         copy.wait_recv()
@@ -370,33 +368,23 @@
         coef[i] = weights[i]
     coef[4] = 1.0 - (weights[0] + weights[1] + weights[2] + weights[3])
 
-    chunks = 4
-    step = levels // chunks
     thi, tlo = tgot_hi[...], tgot_lo[...]
-    sem = 2
-    for c in range(chunks):
-        for src, dst, base in ((pwv, pwo, 0), (sav, sao, levels)):
-            for l in range(c * step, (c + 1) * step):
-                at = base + l
-                field = src[l]
-                sides = neighbours(
-                    field,
-                    halo_rows[at],
-                    pltpu.roll(thi, (LANES - 1 - at) % LANES, 1),
-                    pltpu.roll(tlo, (-at) % LANES, 1),
-                )
-                mixed = coef[4] * field
-                for i in range(4):
-                    mixed = mixed + coef[i] * sides[i]
-                if at == 0:
-                    mixed = mixed - heat[...]
-                dst[l] = mixed
-        for src, dst in ((pwo, pw_out), (sao, sa_out)):
-            cut = slice(c * step, (c + 1) * step)
-            copy = pltpu.make_async_copy(src.at[cut], dst.at[cut], out_sem.at[sem])
-            copy.start()
-            outs.append(copy)
-            sem += 1
+    for src, dst, base in ((pwv, pwo, 0), (sav, sao, levels)):
+        for l in range(levels):
+            at = base + l
+            field = src[l]
+            sides = neighbours(
+                field,
+                halo_rows[at],
+                pltpu.roll(thi, (LANES - 1 - at) % LANES, 1),
+                pltpu.roll(tlo, (-at) % LANES, 1),
+            )
+            mixed = coef[4] * field
+            for i in range(4):
+                mixed = mixed + coef[i] * sides[i]
+            if at == 0:
+                mixed = mixed - heat[...]
+            dst[l] = mixed
 
     for copy in ice_rows + tracer_rows:
         copy.wait_send()
@@ -413,7 +401,21 @@
 
     for copy in patches:
         copy.wait()
-    for copy in outs:
+
+
+def write_out(*refs):
+    *arrays, sems = refs
+    copies = []
+    for src, dst in zip(arrays[:4], arrays[4:]):
+        depth = src.shape[0]
+        parts = 4 if depth % 4 == 0 else 1
+        for i in range(parts):
+            cut = slice(i * depth // parts, (i + 1) * depth // parts)
+            copies.append(
+                pltpu.make_async_copy(src.at[cut], dst.at[cut], sems.at[len(copies)])
+            )
+            copies[-1].start()
+    for copy in copies:
         copy.wait()
 
 
@@ -428,16 +430,17 @@
     f32, i32 = jnp.float32, jnp.int32
     any_space = pl.BlockSpec(memory_space=pl.ANY)
     tile = lambda *shape: pltpu.VMEM(shape, f32)
-    return pl.pallas_call(
+    vmem = pl.BlockSpec(memory_space=pltpu.VMEM)
+    results = pl.pallas_call(
         functools.partial(kernel, n_grp, n_gy, levels, rows, cols, nblock),
         out_shape=(
-            jax.ShapeDtypeStruct(pw.shape, f32),
-            jax.ShapeDtypeStruct(sa.shape, f32),
-            jax.ShapeDtypeStruct(sv.shape, f32),
-            jax.ShapeDtypeStruct(gvs.shape, f32),
+            pltpu.VMEM(pw.shape, f32),
+            pltpu.VMEM(sa.shape, f32),
+            pltpu.VMEM(sv.shape, f32),
+            pltpu.VMEM(gvs.shape, f32),
         ),
         in_specs=[pl.BlockSpec(memory_space=pltpu.SMEM)] + [any_space] * 9,
-        out_specs=(any_space,) * 4,
+        out_specs=(vmem,) * 4,
         scratch_shapes=[
             tile(PLANES, ext, cols + LANES),
             tile(*cc.shape),
@@ -446,10 +449,7 @@
             pltpu.VMEM((rows, cols), i32),
             tile(*pw.shape),
             tile(*sa.shape),
-            tile(*pw.shape),
-            tile(*sa.shape),
             tile(5, rows, cols),
-            tile(2, rows, cols),
             tile(rows, cols),
             pltpu.VMEM((2 * NSUB, cols), i32),
             pltpu.VMEM((8, cols), i32),
@@ -462,10 +462,8 @@
             tile(ext, LANES),
             tile(rows, LANES),
             tile(rows, LANES),
-            tile(5, rows, pair * block_len),
             tile(max(n_gy - 1, 1), 5, rows, pair * block_len),
             pltpu.SemaphoreType.DMA((9,)),
-            pltpu.SemaphoreType.DMA((10,)),
             pltpu.SemaphoreType.DMA((16,)),
             pltpu.SemaphoreType.DMA((16,)),
             pltpu.SemaphoreType.DMA((8,)),
@@ -475,6 +473,13 @@
         ],
         compiler_params=pltpu.CompilerParams(collective_id=0, has_side_effects=True),
     )(home, pw, sa, sv, af, gvs, cc, ct, si, di)
+    return pl.pallas_call(
+        write_out,
+        out_shape=tuple(jax.ShapeDtypeStruct(r.shape, f32) for r in results),
+        in_specs=[vmem] * 4,
+        out_specs=(any_space,) * 4,
+        scratch_shapes=[pltpu.SemaphoreType.DMA((10,))],
+    )(*[pltpu.with_memory_space_constraint(r, pltpu.VMEM) for r in results])
 
 
 def solution(mesh):

time: 21.3 us -> 17.9 us (0.84)
  local copies, waits for them, and re-layouts: 4.35 us -> 0 us
  Pallas kernels: 16.1 us -> 17.1 us
    unnamed x10 -> x0, local copies, waits for them, and re-layouts: 4.35 us -> none
    pallas_call x0 -> x1, Pallas kernels: none -> 1.29 us  [per_device(): pl.pallas_call(write_out, out_shape=tuple((jax.ShapeDtypeStruct(r.shape,...]
where the time goes in v2:
time: 17.9 us; the launch traced here: 17.8 us
  Pallas kernels  17.1 us (96%)
  between operations  0.64 us (4%)
    pallas_call x1, Pallas kernels, per_device(): pl.pallas_call(functools.partial(kernel, n_grp, n_gy, levels, rows, cols,...  15.9 us
    pallas_call x1, Pallas kernels, per_device(): pl.pallas_call(write_out, out_shape=tuple((jax.ShapeDtypeStruct(r.shape,...  1.29 us

profile of v2, /device:TPU:0, one launch (start us, length us, event | category | flops | bytes accessed | tf_op | source)
XLA Modules:
  0.0 17.8 jit_solution(13846096826660275004)
XLA Ops:
  0.6 15.9 %shard_map.129 = (f32[24,16,512]{2,1,0:T(8,128)S(1)}, f32[24,16,512]{2,1,0:T(8,128)S(1)}, f32[2,16,512]{2,1,0:T(8,128)S(1)}, f32[5,16,512]{2,1,0:T(8,128)S(1)}) custom-call(s32[1,4]{1,0:T(1,128)} %home.1, f32[24,16,512]{2,1,0:T(8,128)} %pw.1, f32[24,16,512]{2,1,0:T(8,128)} %sa.1, f32[2,16,512]{2,1,0:T(8,128)} %sv.1, f32[2,16,512]{2,1,0:T(8,128)} %af.1, ...), custom_call_target="tpu_custom_call" | custom-call | tf_op jit(solution)/shard_map/pallas_call | solution.py:434
  16.5 1.3 %shard_map.130 = (f32[24,16,512]{2,1,0:T(8,128)}, f32[24,16,512]{2,1,0:T(8,128)}, f32[2,16,512]{2,1,0:T(8,128)}, f32[5,16,512]{2,1,0:T(8,128)}) custom-call(f32[24,16,512]{2,1,0:T(8,128)S(1)} %get-tuple-element.8.refs_0_, f32[24,16,512]{2,1,0:T(8,128)S(1)} %get-tuple-element.9.refs_1_, f32[2,16,512]{2,1,0:T(8,128)S(1)} %get-tuple-element.10.refs_2_, ...), custom_call_target="tpu_custom_call" | custom-call | tf_op jit(solution)/shard_map/pallas_call | solution.py:476

commit v3 on v2

--- a/solution.py
+++ b/solution.py
@@ -34,13 +34,13 @@
 
 def kernel(
     n_grp, n_gy, levels, rows, cols, nblock,
-    home, pw, sa, sv, af, gvs, cc, ct, si, di,
+    home_hbm, pw, sa, sv, af, gvs, cc, ct, si, di,
     pwo, sao, cvel, glac_out,
     win, ccv, ctv, siv, div_, pwv, sav, coef, heat,
-    icy_rows, wet_rows, halo_rows,
+    wet_rows, halo_rows,
     pack_hi, pack_lo, tpack_hi, tpack_lo, got_hi, got_lo, tgot_hi, tgot_lo,
     picks,
-    in_sem, row_send, row_recv, col_send, col_recv, patch_send, patch_recv,
+    home, in_sem, row_send, row_recv, col_send, col_recv, patch_send, patch_recv,
 ):
     g = lax.axis_index("grp")
     y = lax.axis_index("gy")
@@ -51,6 +51,31 @@
     ext = rows + 2 * NSUB
     block_len = cols // nblock
     pair = nblock // n_gy
+
+    barrier = pltpu.get_barrier_semaphore()
+
+    def greet(gg, yy):
+        pl.semaphore_signal(
+            barrier, inc=1, device_id={"grp": gg, "gy": yy},
+            device_id_type=pl.DeviceIdType.MESH,
+        )
+
+    greet(east, y)
+    greet(west, y)
+    for k in range(1, n_gy):
+        greet(g, lax.rem(y + k, n_gy))
+
+    @pl.when(has_up)
+    def _():
+        greet(east, y + 1)
+        greet(west, y + 1)
+
+    @pl.when(has_dn)
+    def _():
+        greet(east, y - 1)
+        greet(west, y - 1)
+
+    both = jnp.where(has_up, 2, 0) + jnp.where(has_dn, 2, 0)
 
     center = (slice(0, rows), slice(0, cols))
     loads = [
@@ -66,36 +91,12 @@
                 (af, win.at[7:9, 0:rows, 0:cols]),
                 (pw, pwv),
                 (sa, sav),
+                (home_hbm, home),
             )
         )
     ]
-    for load in loads:
+    for load in loads[:7]:
         load.start()
-
-    barrier = pltpu.get_barrier_semaphore()
-
-    def greet(gg, yy):
-        pl.semaphore_signal(
-            barrier, inc=1, device_id={"grp": gg, "gy": yy},
-            device_id_type=pl.DeviceIdType.MESH,
-        )
-
-    greet(east, y)
-    greet(west, y)
-    for k in range(1, n_gy):
-        greet(g, lax.rem(y + k, n_gy))
-
-    @pl.when(has_up)
-    def _():
-        greet(east, y + 1)
-        greet(west, y + 1)
-
-    @pl.when(has_dn)
-    def _():
-        greet(east, y - 1)
-        greet(west, y - 1)
-
-    both = jnp.where(has_up, 2, 0) + jnp.where(has_dn, 2, 0)
 
     for load in loads[:4]:
         load.wait()
@@ -105,27 +106,8 @@
     wet = siv[...].astype(jnp.float32)
     for load in loads[4:7]:
         load.wait()
-
-    lane16 = lax.broadcasted_iota(jnp.int32, (rows, LANES), 1)
-
-    def pack(entries):
-        out = jnp.zeros((rows, LANES), jnp.float32)
-        for tile, first, place, width in entries:
-            moved = pltpu.roll(tile, (place - first) % LANES, 1)
-            out = jnp.where((lane16 >= place) & (lane16 < place + width), moved, out)
-        return out
-
-    wet_lane = PLANES * NSUB
-    hi = slice(cols - LANES, cols)
-    lo = slice(0, LANES)
-    pack_hi[...] = pack(
-        [(win[p, 0:rows, hi], LANES - NSUB, NSUB * p, NSUB) for p in range(PLANES)]
-        + [(wet[:, hi], LANES - 1, wet_lane, 1)]
-    )
-    pack_lo[...] = pack(
-        [(win[p, 0:rows, lo], 0, NSUB * p, NSUB) for p in range(PLANES)]
-        + [(wet[:, lo], 0, wet_lane, 1)]
-    )
+    for load in loads[7:]:
+        load.start()
 
     pl.semaphore_wait(barrier, 1 + n_gy + both)
 
@@ -143,14 +125,7 @@
     ):
         src_rows = slice(first, first + NSUB)
         dst_rows = slice(at, at + NSUB)
-        ice_pairs = (
-            (gvs.at[:, src_rows, :], win.at[0:5, dst_rows, 0:cols]),
-            (sv.at[:, src_rows, :], win.at[5:7, dst_rows, 0:cols]),
-            (af.at[:, src_rows, :], win.at[7:9, dst_rows, 0:cols]),
-            (win.at[A_PLANE : H_PLANE + 1, src_rows, 0:cols],
-             win.at[A_PLANE : H_PLANE + 1, dst_rows, 0:cols]),
-            (di.at[src_rows, :], icy_rows.at[at - rows : at - rows + NSUB, :]),
-        )
+        ice_pairs = ((win.at[:, src_rows, 0:cols], win.at[:, dst_rows, 0:cols]),)
         tracer_pairs = (
             (si.at[edge : edge + 1, :], wet_rows.at[sub : sub + 1, :]),
             (pw.at[:, edge : edge + 1, :], halo_rows.at[0:levels, sub : sub + 1, :]),
@@ -180,20 +155,41 @@
     tr_up = remote(tpack_hi, tgot_lo, col_send.at[6], col_recv.at[6], g, y + 1)
     tr_dn = remote(tpack_lo, tgot_hi, col_send.at[7], col_recv.at[7], g, y - 1)
 
+    lane16 = lax.broadcasted_iota(jnp.int32, (rows, LANES), 1)
+
+    def pack(entries):
+        out = jnp.zeros((rows, LANES), jnp.float32)
+        for tile, first, place, width in entries:
+            moved = pltpu.roll(tile, (place - first) % LANES, 1)
+            out = jnp.where((lane16 >= place) & (lane16 < place + width), moved, out)
+        return out
+
+    wet_lane = PLANES * NSUB
+    hi = slice(cols - LANES, cols)
+    lo = slice(0, LANES)
+    pack_hi[...] = pack(
+        [(win[p, 0:rows, hi], LANES - NSUB, NSUB * p, NSUB) for p in range(PLANES)]
+        + [(wet[:, hi], LANES - 1, wet_lane, 1)]
+    )
+    pack_lo[...] = pack(
+        [(win[p, 0:rows, lo], 0, NSUB * p, NSUB) for p in range(PLANES)]
+        + [(wet[:, lo], 0, wet_lane, 1)]
+    )
+
     @pl.when(has_up)
     def _():
-        for copy in ice_up:
+        for copy in ice_up[1:] + ice_up[:1]:
             copy.start()
 
     @pl.when(has_dn)
     def _():
-        for copy in ice_dn:
+        for copy in ice_dn[1:] + ice_dn[:1]:
             copy.start()
 
     for copy in tracer_rows:
         copy.start()
 
-    for load in loads[7:]:
+    for load in loads[7:9]:
         load.wait()
     for out, cut, first in ((tpack_hi, hi, LANES - 1), (tpack_lo, lo, 0)):
         out[...] = pack(
@@ -226,28 +222,33 @@
         got_lo[...] = jnp.zeros_like(got_lo)
         tgot_lo[...] = jnp.zeros_like(tgot_lo)
 
+    def unpack(first, last):
+        lane = lax.broadcasted_iota(jnp.int32, (last - first, LANES), 1)
+        from_hi, from_lo = got_hi[first:last, :], got_lo[first:last, :]
+        for p in range(PLANES):
+            high = pltpu.roll(from_hi, (-NSUB * p) % LANES, 1)
+            low = pltpu.roll(from_lo, (LANES - NSUB - NSUB * p) % LANES, 1)
+            win[p, first:last, cols : cols + LANES] = jnp.where(
+                lane < NSUB, high, jnp.where(lane >= LANES - NSUB, low, 0.0)
+            )
+
+    def columns(part):
+        @pl.when(has_up)
+        def _():
+            for copy in ice_dn[part]:
+                copy.wait_recv()
+
+        @pl.when(has_dn)
+        def _():
+            for copy in ice_up[part]:
+                copy.wait_recv()
+
+    columns(slice(0, 1))
+    unpack(0, rows)
+    columns(slice(1, 3))
+    unpack(rows, ext)
     for copy in ice_rows:
         copy.wait_recv()
-
-    @pl.when(has_up)
-    def _():
-        for copy in ice_dn:
-            copy.wait_recv()
-
-    @pl.when(has_dn)
-    def _():
-        for copy in ice_up:
-            copy.wait_recv()
-
-    win[ICY_PLANE, rows:ext, 0:cols] = icy_rows[...].astype(jnp.float32)
-    lane24 = lax.broadcasted_iota(jnp.int32, (ext, LANES), 1)
-    from_hi, from_lo = got_hi[...], got_lo[...]
-    for p in range(PLANES):
-        high = pltpu.roll(from_hi, (-NSUB * p) % LANES, 1)
-        low = pltpu.roll(from_lo, (LANES - NSUB - NSUB * p) % LANES, 1)
-        win[p, :, cols : cols + LANES] = jnp.where(
-            lane24 < NSUB, high, jnp.where(lane24 >= LANES - NSUB, low, 0.0)
-        )
 
     vel_u, vel_v = win[0], win[1]
     sig_one, sig_two, sig_shear = win[2], win[3], win[4]
@@ -294,6 +295,7 @@
 
     state = [f[0:rows, 0:cols] for f in (vel_u, vel_v, sig_one, sig_two, sig_shear)]
 
+    loads[9].wait()
     homes = [home[0, b] for b in range(nblock)]
 
     def choose(slot, field):
@@ -439,7 +441,7 @@
             pltpu.VMEM(sv.shape, f32),
             pltpu.VMEM(gvs.shape, f32),
         ),
-        in_specs=[pl.BlockSpec(memory_space=pltpu.SMEM)] + [any_space] * 9,
+        in_specs=[any_space] * 10,
         out_specs=(vmem,) * 4,
         scratch_shapes=[
             tile(PLANES, ext, cols + LANES),
@@ -451,7 +453,6 @@
             tile(*sa.shape),
             tile(5, rows, cols),
             tile(rows, cols),
-            pltpu.VMEM((2 * NSUB, cols), i32),
             pltpu.VMEM((8, cols), i32),
             tile(2 * levels, 8, cols),
             tile(rows, LANES),
@@ -463,9 +464,10 @@
             tile(rows, LANES),
             tile(rows, LANES),
             tile(max(n_gy - 1, 1), 5, rows, pair * block_len),
-            pltpu.SemaphoreType.DMA((9,)),
-            pltpu.SemaphoreType.DMA((16,)),
-            pltpu.SemaphoreType.DMA((16,)),
+            pltpu.SMEM(home.shape, i32),
+            pltpu.SemaphoreType.DMA((10,)),
+            pltpu.SemaphoreType.DMA((8,)),
+            pltpu.SemaphoreType.DMA((8,)),
             pltpu.SemaphoreType.DMA((8,)),
             pltpu.SemaphoreType.DMA((8,)),
             pltpu.SemaphoreType.DMA((max(n_gy - 1, 1),)),

time: 17.9 us -> 17 us (0.950)
  Pallas kernels: 17.1 us -> 16.2 us
    pallas_call x1, Pallas kernels: 15.9 us -> 14.9 us  [per_device(): pl.pallas_call(functools.partial(kernel, n_grp, n_gy, levels, rows, cols,...]
where the time goes in v3:
time: 17 us; the launch traced here: 16.8 us
  Pallas kernels  16.2 us (95%)
  between operations  0.64 us (4%)
    pallas_call x1, Pallas kernels, per_device(): pl.pallas_call(functools.partial(kernel, n_grp, n_gy, levels, rows, cols,...  14.9 us
    pallas_call x1, Pallas kernels, per_device(): pl.pallas_call(write_out, out_shape=tuple((jax.ShapeDtypeStruct(r.shape,...  1.29 us

profile of v3, /device:TPU:0, one launch (start us, length us, event | category | flops | bytes accessed | tf_op | source)
XLA Modules:
  0.0 16.8 jit_solution(16381816109675260734)
XLA Ops:
  0.6 14.9 %shard_map.129 = (f32[24,16,512]{2,1,0:T(8,128)S(1)}, f32[24,16,512]{2,1,0:T(8,128)S(1)}, f32[2,16,512]{2,1,0:T(8,128)S(1)}, f32[5,16,512]{2,1,0:T(8,128)S(1)}) custom-call(s32[1,4]{1,0:T(1,128)} %home_hbm.1, f32[24,16,512]{2,1,0:T(8,128)} %pw.1, f32[24,16,512]{2,1,0:T(8,128)} %sa.1, f32[2,16,512]{2,1,0:T(8,128)} %sv.1, f32[2,16,512]{2,1,0:T(8,128)} %af.1, ...), custom_call_target="tpu_custom_call" | custom-call | tf_op jit(solution)/shard_map/pallas_call | solution.py:436
  15.5 1.3 %shard_map.130 = (f32[24,16,512]{2,1,0:T(8,128)}, f32[24,16,512]{2,1,0:T(8,128)}, f32[2,16,512]{2,1,0:T(8,128)}, f32[5,16,512]{2,1,0:T(8,128)}) custom-call(f32[24,16,512]{2,1,0:T(8,128)S(1)} %get-tuple-element.8.refs_0_, f32[24,16,512]{2,1,0:T(8,128)S(1)} %get-tuple-element.9.refs_1_, f32[2,16,512]{2,1,0:T(8,128)S(1)} %get-tuple-element.10.refs_2_, ...), custom_call_target="tpu_custom_call" | custom-call | tf_op jit(solution)/shard_map/pallas_call | solution.py:478
